TPU v7x, 32 devices: a whole 2x2x4 slice. The times are simulated.
32 devices in a mesh: segment: 4 (over y, x), region: 8 (over z, core).
Axes of the slice: x: 2, y: 2, z: 4, core: 2. Of those that a mesh axis runs over, the one named last changes fastest.
Arguments:
- features: bfloat16 [4, 2048, 512], P('segment', 'region'), may hold values from -6 to 6
- edge_weights: bfloat16 [4, 16, 3, 128, 128], P('segment', 'region'), may hold values from -4 to 4
- adjacency: int32 [4, 16, 3], P('segment', 'region'), may hold values from 0 to 3, as said below
- counts: int32 [4, 8], P('segment'), may hold values from 128 to 256, as said below
- weight_self: bfloat16 [4, 512, 512], P('segment'), may hold values from -0.25 to 0.25
- weight_neighbour: bfloat16 [4, 512, 512], P('segment'), may hold values from -0.25 to 0.25
- cotangent: bfloat16 [4, 2048, 512], P('segment', 'region'), may hold values from -6 to 6
Outputs:
- final_hidden: bfloat16 [4, 2048, 512], P('segment', 'region')
- input_grad: bfloat16 [4, 2048, 512], P('segment', 'region')
- grad_self: float32 [4, 512, 512], P('segment')
- grad_neighbour: float32 [4, 512, 512], P('segment')
Inputs may be any that keep to these rules, and one draw needn't show every extreme that they name: `adjacency`: each row names 3 distinct extended positions; the row of a block at own position p includes p; the row of a region's first block includes position 0 and that of its last block includes the last extended position. `counts`: in every event some region holds exactly 256 real hits.
All inputs are finite; a program needn't handle non-finite values.
Results may differ from a plain program's by a relative error of at most 0.018.
Values may be sent and summed in bfloat16 or wider, within the bound.
A program may use at most 64 MiB of HBM per device.

v0:
```python
import functools
import math

import jax
import jax.numpy as jnp
from jax import lax
from jax.experimental import pallas as pl
from jax.experimental.pallas import tpu as pltpu
from jax.sharding import PartitionSpec as P

BF = jnp.bfloat16
LAG = 1
F32 = jnp.float32


def mm(a, b, ca, cb):
    return lax.dot_general(a, b, (((ca,), (cb,)), ((), ())), preferred_element_type=F32)


def kernel(
    S, R, adj, cnt, feat, edge, ws, wn, cot, final, igrad, gs, gn,
    w, cotv, hn, pre, fh, bs, bh, slope, pact, pslope, gsend, srecv, zs, zrecv, zg, mv, pm,
    a_own, a_halo, inv_ref, mask_ref,
    loc_sem, ww_s, ww_r, wp_s, wp_r, fh_s, fh_r, bh_s, bh_r, pa_s, pa_r, ps_s, ps_r,
    sg_s, sg_r, zr_s, zr_r, zg_s, zg_r, mv_s, mv_r, pm_s, pm_r,
):
    L, Z = S, R // 2
    BLK = edge.shape[-1]
    ROWS, D = feat.shape
    CH = D // S
    Q, DQ = zs.shape[1], D // zs.shape[1]
    pr, pc = zs.shape[3:]
    cols = DQ // pc
    HD = D // 2
    s, r = lax.axis_index("segment"), lax.axis_index("region")
    z, c = r // 2, r % 2
    left, right = (r + R - 1) % R, (r + 1) % R
    partner = r + 1 - 2 * c
    sx, sy = s + 1 - 2 * (s % 2), s + 2 - 4 * (s // 2)

    def rc(src, dst, ss, rs, dev):
        return pltpu.make_async_remote_copy(
            src_ref=src, dst_ref=dst, send_sem=ss, recv_sem=rs,
            device_id=dev, device_id_type=pl.DeviceIdType.MESH,
        )

    pending = []

    def go(cp):
        cp.start()
        pending.append(cp)
        return cp

    own_w = [
        pltpu.make_async_copy(ws, w.at[s, 0], loc_sem.at[0]),
        pltpu.make_async_copy(wn, w.at[s, 1], loc_sem.at[1]),
    ]
    own_cot = pltpu.make_async_copy(cot, cotv, loc_sem.at[2])
    for cp in own_w:
        cp.start()
    own_cot.start()

    barrier = pltpu.get_barrier_semaphore()
    greet = [(s, left), (s, right)]
    greet += [((s + k) % S, r) for k in range(1, S)]
    greet += [(s, (r + 2 * k) % R) for k in range(1, Z)]
    for dev in greet:
        pl.semaphore_signal(barrier, inc=1, device_id=dev, device_id_type=pl.DeviceIdType.MESH)

    limit = cnt[0, r]
    rows = lax.broadcasted_iota(jnp.int32, (ROWS, D), 0)
    mask_ref[...] = (rows < limit).astype(F32)
    mask = lambda: mask_ref[...]
    h0 = jnp.where(mask() > 0, feat[...], jnp.zeros((ROWS, D), BF))
    hn[0, 0] = h0
    pl.semaphore_wait(barrier, len(greet))

    def halo_send(l):
        go(rc(hn.at[l, 0, pl.ds(ROWS - BLK, BLK)], fh.at[l, pl.ds(0, BLK)],
              fh_s.at[l, 0], fh_r.at[l, 0], (s, right)))
        go(rc(hn.at[l, 0, pl.ds(0, BLK)], fh.at[l, pl.ds(BLK, BLK)],
              fh_s.at[l, 1], fh_r.at[l, 1], (s, left)))

    def halo_wait(l, buf, rs):
        for i in range(2):
            part = buf.at[l, pl.ds(i * BLK, BLK)]
            rc(part, part, rs.at[l, i], rs.at[l, i], (s, left)).wait_recv()

    halo_send(0)
    for cp in own_w:
        cp.wait()

    def half(l, h):
        return w.at[l, c, pl.ds(h * HD, HD)]

    def w_send(h, to, i):
        return rc(half(s, h), half(s, h), ww_s.at[i], ww_r.at[s, h], (to, r))

    first = [w_send(0, sx, 0), w_send(1, sy, 1)]
    second = [w_send(1, sx, 2), w_send(0, sy, 3)]
    for cp in first:
        go(cp)

    @pl.when(s == 0)
    def _():
        for cp in second:
            cp.start()

    for b in range(2):
        blk = pl.ds(b * BLK, BLK)
        tiles = [edge[b, k] for k in range(3)]
        sq = sum(jnp.sum(jnp.square(t.astype(F32)), axis=1, keepdims=True) for t in tiles)
        inv_ref[blk, :] = jnp.broadcast_to(1.0 / (1.0 + jnp.sqrt(sq)), (BLK, D))
        for m in range(4):
            part = jnp.zeros((BLK, BLK), F32)
            for k in range(3):
                part = jnp.where(adj[b, k] == m, tiles[k].astype(F32), part)
            part = part.astype(BF)
            if m == 0:
                a_halo[blk, pl.ds(0, BLK)] = part
            elif m == 3:
                a_halo[blk, pl.ds(BLK, BLK)] = part
            else:
                a_own[blk, pl.ds((m - 1) * BLK, BLK)] = part

    def w_recv(l, h):
        rc(half(l, h), half(l, h), ww_s.at[0], ww_r.at[l, h], (s, partner)).wait_recv()

    def to_partner(l, h):
        return rc(half(l, h), half(l, h), wp_s.at[l, h], wp_r.at[l, h], (s, partner))

    def relays():
        for l, h, to, i in ((sx, 0, sy, 4), (sy, 1, sx, 5)):
            w_recv(l, h)
            go(rc(half(l, h), half(l, h), ww_s.at[i], ww_r.at[l, h], (to, r)))
            go(to_partner(l, h))

        @pl.when(s != 0)
        def _():
            for cp in second:
                cp.start()

        pending.extend(second)

    def w_forward(l):
        for h in range(2):
            @pl.when((s != l) & ((sx, sy)[h] != l))
            def _():
                w_recv(l, h)
                to_partner(l, h).start()

    def w_wait(l):
        @pl.when(s != l)
        def _():
            for h in range(2):
                src = w.at[l, 1 - c, pl.ds(h * HD, HD)]
                rc(src, src, wp_s.at[l, h], wp_r.at[l, h], (s, partner)).wait_recv()

    for l in range(L):
        own = mm(a_own[...], hn[l, 0], 1, 0)
        if l == 0:
            relays()
            w_forward(0)
            w_wait(0)
        selfp = mm(hn[l, 0], w[l, 0], 1, 0)
        halo_wait(l, fh, fh_r)
        nbr = ((own + mm(a_halo[...], fh[l], 1, 0)) * inv_ref[...]).astype(BF)
        hn[l, 1] = nbr
        p = selfp + mm(nbr, w[l, 1], 1, 0)
        pre[l] = p
        out = hn[l, 0].astype(F32) + p * jax.nn.sigmoid(p)
        nxt = (mask() * out).astype(BF)
        if l + 1 < L:
            hn[l + 1, 0] = nxt
            halo_send(l + 1)
            w_forward(l + 1)
            go(rc(hn.at[l, 1 - c], pact.at[l], pa_s.at[l], pa_r.at[l], (s, partner)))
            w_wait(l + 1)
        else:
            final[...] = nxt
            go(rc(hn.at[l, 1 - c], pact.at[l], pa_s.at[l], pa_r.at[l], (s, partner)))

    def stage_b(l):
        rc(pact.at[l], pact.at[l], pa_s.at[l], pa_r.at[l], (s, partner)).wait_recv()
        rc(pslope.at[l], pslope.at[l], ps_s.at[l], ps_r.at[l], (s, partner)).wait_recv()
        for q in range(Q):
            cs = pl.ds(q * DQ, DQ)
            g = mm(hn[l, c], slope[l, :, cs], 0, 0) + mm(pact[l], pslope[l, :, cs], 0, 0)
            gsend[l, q] = g.reshape(S, CH, DQ).astype(BF)
            for k in range(1, S):
                go(rc(gsend.at[l, q, (s + k) % S], srecv.at[l, q, k - 1],
                      sg_s.at[l, q, k - 1], sg_r.at[l, q, k - 1], ((s + k) % S, r)))

    def stage_c(l, q):
        acc = gsend[l, q, s].astype(F32)
        for k in range(1, S):
            x = srecv.at[l, q, k - 1]
            rc(x, x, sg_s.at[l, q, k - 1], sg_r.at[l, q, k - 1], ((s + k) % S, r)).wait_recv()
            acc = acc + srecv[l, q, k - 1].astype(F32)
        acc = acc.astype(BF)
        for i in range(Z):
            a, b = (i // cols) * pr, (i % cols) * pc
            zs[l, q, i] = acc[a:a + pr, b:b + pc]
        for k in range(1, Z):
            go(rc(zs.at[l, q, (z + k) % Z], zrecv.at[l, q, k - 1],
                  zr_s.at[l, q, k - 1], zr_r.at[l, q, k - 1], (s, (r + 2 * k) % R)))

    def stage_d(l, q):
        acc = zs[l, q, z].astype(F32)
        for k in range(1, Z):
            x = zrecv.at[l, q, k - 1]
            rc(x, x, zr_s.at[l, q, k - 1], zr_r.at[l, q, k - 1], (s, (r + 2 * k) % R)).wait_recv()
            acc = acc + zrecv[l, q, k - 1].astype(F32)
        zg[l, q, z] = acc.astype(BF)
        for k in range(1, Z):
            go(rc(zg.at[l, q, z], zg.at[l, q, z],
                  zg_s.at[l, q, k - 1], zg_r.at[l, q, k - 1], (s, (r + 2 * k) % R)))

    def move(l, q):
        i = (l - s + S) % S
        return rc(zg.at[l, q], mv.at[s, q], mv_s.at[q, i], mv_r.at[q, i], (l, r))

    def stage_e(l, q):
        for k in range(1, Z):
            x = zg.at[l, q, (z + Z - k) % Z]
            rc(x, x, zg_s.at[l, q, k - 1], zg_r.at[l, q, k - 1], (s, (r + 2 * k) % R)).wait_recv()

        @pl.when(s != l)
        def _():
            move(l, q).start()

    def stage(f, l):
        if l < L:
            for q in range(Q):
                f(l, q)

    own_cot.wait()
    grad = cotv[...].astype(F32)
    for l in reversed(range(L)):
        masked = mask() * grad
        p = pre[l]
        sg = jax.nn.sigmoid(p)
        sl = (masked * (sg * (1.0 + p * (1.0 - sg)))).astype(BF)
        slope[l] = sl
        go(rc(slope.at[l], pslope.at[l], ps_s.at[l], ps_r.at[l], (s, partner)))
        scaled = (mm(sl, w[l, 1], 1, 1) * inv_ref[...]).astype(BF)
        bs[l] = mm(a_halo[...], scaled, 0, 0).astype(BF)
        go(rc(bs.at[l, pl.ds(0, BLK)], bh.at[l, pl.ds(BLK, BLK)],
              bh_s.at[l, 0], bh_r.at[l, 1], (s, left)))
        go(rc(bs.at[l, pl.ds(BLK, BLK)], bh.at[l, pl.ds(0, BLK)],
              bh_s.at[l, 1], bh_r.at[l, 0], (s, right)))
        total = masked + mm(sl, w[l, 0], 1, 1) + mm(a_own[...], scaled, 0, 0)
        stage_b(l)
        stage(stage_c, l + LAG)
        stage(stage_d, l + LAG + 1)
        stage(stage_e, l + LAG + 2)
        halo_wait(l, bh, bh_r)
        grad = (total + bh[l].astype(F32)).astype(BF).astype(F32)
    igrad[...] = (mask() * grad).astype(BF)

    for l in range(-1, -LAG - 3, -1):
        for f, m in ((stage_e, l + LAG + 2), (stage_d, l + LAG + 1), (stage_c, l + LAG)):
            if 0 <= m:
                stage(f, m)

    def pair(k, q):
        x = (s + S - k) % S
        return rc(mv.at[x, q], pm.at[x, q], pm_s.at[q, k], pm_r.at[q, k], (s, partner))

    for q in range(Q):
        mv[s, q] = zg[s, q]
        go(pair(0, q))
        for k in range(1, S):
            x = mv.at[(s + S - k) % S, q]
            rc(x, x, mv_s.at[q, k], mv_r.at[q, k], (s, partner)).wait_recv()
            go(pair(k, q))
    for q in range(Q):
        for k in range(S):
            pair(k, q).wait_recv()
    for q in range(Q):
        for k in range(S):
            for i in range(Z):
                a, b = k * CH + (i // cols) * pr, q * DQ + (i % cols) * pc
                mine, other = mv[k, q, i], pm[k, q, i]
                gs[pl.ds(a, pr), pl.ds(b, pc)] = jnp.where(c == 0, mine, other)
                gn[pl.ds(a, pr), pl.ds(b, pc)] = jnp.where(c == 0, other, mine)
    for cp in pending:
        cp.wait_send()
    for l in range(L):
        @pl.when(s != l)
        def _():
            for q in range(Q):
                move(l, q).wait_send()
        for h in range(2):
            @pl.when((s != l) & ((sx, sy)[h] != l))
            def _():
                to_partner(l, h).wait_send()


def body(features, edge_weights, adjacency, counts, weight_self, weight_neighbour, cotangent):
    R, S = lax.axis_size("region"), lax.axis_size("segment")
    rows, D = features.shape[1:]
    blk = edge_weights.shape[3]
    L, Z, CH = S, R // 2, D // S
    Q = 2 if Z <= CH // 16 else 1
    rg = min(Z, CH // 16)
    cg = Z // rg
    pr, pc = CH // rg, D // Q // cg
    scale = 1.0 / math.sqrt(S * features.shape[0] * rows * R)
    V = pltpu.VMEM
    DMA = pltpu.SemaphoreType.DMA
    vm = pl.BlockSpec(memory_space=pltpu.VMEM)
    sm = pl.BlockSpec(memory_space=pltpu.SMEM)
    anys = pl.BlockSpec(memory_space=pl.ANY)
    sems = [DMA((3,))]
    for shape in [((6,), (L, 2)), ((L, 2),) * 2, ((L, 2),) * 2, ((L, 2),) * 2, ((L,),) * 2, ((L,),) * 2,
                  ((L, Q, S - 1),) * 2, ((L, Q, Z - 1),) * 2, ((L, Q, Z - 1),) * 2, ((Q, S),) * 2, ((Q, S),) * 2]:
        sems += [DMA(shape[0]), DMA(shape[1])]
    final, igrad, gs, gn = pl.pallas_call(
        functools.partial(kernel, S, R),
        out_shape=(
            jax.ShapeDtypeStruct((rows, D), BF),
            jax.ShapeDtypeStruct((rows, D), BF),
            jax.ShapeDtypeStruct((D, D), BF),
            jax.ShapeDtypeStruct((D, D), BF),
        ),
        in_specs=[sm, sm, vm, vm, anys, anys, anys],
        out_specs=(vm, vm, vm, vm),
        scratch_shapes=[
            V((S, 2, D, D), BF), V((rows, D), BF), V((L, 2, rows, D), BF), V((L, rows, D), F32),
            V((L, 2 * blk, D), BF), V((L, 2 * blk, D), BF), V((L, 2 * blk, D), BF),
            V((L, rows, D), BF), V((L, rows, D), BF), V((L, rows, D), BF),
            V((L, Q, S, CH, D // Q), BF), V((L, Q, S - 1, CH, D // Q), BF),
            V((L, Q, Z, pr, pc), BF), V((L, Q, Z - 1, pr, pc), BF), V((L, Q, Z, pr, pc), BF),
            V((S, Q, Z, pr, pc), BF), V((S, Q, Z, pr, pc), BF),
            V((rows, 2 * blk), BF), V((rows, 2 * blk), BF), V((rows, D), F32), V((rows, D), F32),
        ] + sems,
        compiler_params=pltpu.CompilerParams(
            collective_id=0, has_side_effects=True, vmem_limit_bytes=60 * 1024 * 1024
        ),
        name="network",
    )(adjacency[0], counts, features[0], edge_weights[0], weight_self[0], weight_neighbour[0], cotangent[0])
    return (final[None], igrad[None], gs[None].astype(F32) * scale, gn[None].astype(F32) * scale)


def solution(mesh):
    in_specs = (
        P("segment", "region", None),
        P("segment", "region", None, None, None),
        P("segment", "region", None),
        P("segment", None),
        P("segment", None, None),
        P("segment", None, None),
        P("segment", "region", None),
    )
    out_specs = (
        P("segment", "region", None),
        P("segment", "region", None),
        P("segment", None, None),
        P("segment", None, None),
    )
    return jax.shard_map(body, mesh=mesh, in_specs=in_specs, out_specs=out_specs, check_vma=False)
```

profile of v0, /device:TPU:1, one launch (start us, length us, event | category | flops | bytes accessed | tf_op | source)
XLA Modules:
  0.0 96.9 jit_solution(17736151344829637075)
XLA Ops:
  0.6 91.7 %network.1 = (bf16[256,512]{1,0:T(8,128)(2,1)}, bf16[256,512]{1,0:T(8,128)(2,1)}, bf16[512,512]{1,0:T(8,128)(2,1)}, bf16[512,512]{1,0:T(8,128)(2,1)}) custom-call(s32[2,3]{1,0:T(2,128)} %bitcast.19, s32[1,8]{1,0:T(1,128)} %cnt.1, bf16[256,512]{1,0:T(8,128)(2,1)} %bitcast.14, bf16[2,3,128,128]{3,2,1,0:T(8,128)(2,1)} %bitcast.18, bf16[512,512]{1,0:T(8,128)(2,1)} %bitcast.12, ...), custom_call_target="tpu_custom_call" | custom-call | tf_op jit(solution)/shard_map/network/pallas_call | solution.py:319
  92.3 0.0 copy-start.1
  92.3 2.9 %multiply_bitcast_fusion = (f32[1,512,512]{2,1,0:T(8,128)}, f32[1,512,512]{2,1,0:T(8,128)}) fusion(bf16[512,512]{1,0:T(8,128)(2,1)} %get-tuple-element.11, bf16[512,512]{1,0:T(8,128)(2,1)} %get-tuple-element.10), kind=kLoop, calls=%fused_computation | loop fusion | flops 1048576 | bytes 3145728 | tf_op jit(solution)/shard_map/mul | solution.py:343
  95.2 0.0 copy-done.1
  95.2 0.0 copy-start
  95.2 0.7 copy.13
  95.9 0.3 copy-done
  96.2 0.7 copy.14
Async XLA Ops:
  92.3 2.9 %copy-start.1 = (bf16[256,512]{1,0:T(8,128)(2,1)S(1)}, bf16[256,512]{1,0:T(8,128)(2,1)}, u32[]{:S(2)}) copy-start(bf16[256,512]{1,0:T(8,128)(2,1)} %get-tuple-element.8) | copy-start | bytes 786436
  95.2 1.0 %copy-start = (bf16[256,512]{1,0:T(8,128)(2,1)S(1)}, bf16[256,512]{1,0:T(8,128)(2,1)}, u32[]{:S(2)}) copy-start(bf16[256,512]{1,0:T(8,128)(2,1)} %get-tuple-element.9) | copy-start | bytes 786436
where the time goes:
time: 97.1 us; the launch traced here: 96.9 us
  Pallas kernels  91.7 us (94%)
  other arithmetic  2.85 us (3%)
  local copies, waits for them, and re-layouts  1.75 us (2%)
    pallas_call x1, Pallas kernels, body(): pl.pallas_call(functools.partial(kernel, S, R), out_shape=(jax.ShapeDtype...  91.7 us
    mul x1, other arithmetic, body(): gn[None].astype(F32) * scale  2.85 us

commit v1 on v0

--- a/solution.py
+++ b/solution.py
@@ -10,6 +10,7 @@
 
 BF = jnp.bfloat16
 LAG = 1
+PARTS = 4
 F32 = jnp.float32
 
 
@@ -18,8 +19,8 @@
 
 
 def kernel(
-    S, R, adj, cnt, feat, edge, ws, wn, cot, final, igrad, gs, gn,
-    w, cotv, hn, pre, fh, bs, bh, slope, pact, pslope, gsend, srecv, zs, zrecv, zg, mv, pm,
+    S, R, adj, cnt, feat_in, edge_in, ws, wn, cot, final, igrad, gs, gn,
+    feat, edge, w, cotv, hn, pre, fh, bs, bh, slope, pact, pslope, gsend, srecv, zs, zrecv, zg, mv, pm,
     a_own, a_halo, inv_ref, mask_ref,
     loc_sem, ww_s, ww_r, wp_s, wp_r, fh_s, fh_r, bh_s, bh_r, pa_s, pa_r, ps_s, ps_r,
     sg_s, sg_r, zr_s, zr_r, zg_s, zg_r, mv_s, mv_r, pm_s, pm_r,
@@ -56,9 +57,8 @@
         pltpu.make_async_copy(wn, w.at[s, 1], loc_sem.at[1]),
     ]
     own_cot = pltpu.make_async_copy(cot, cotv, loc_sem.at[2])
-    for cp in own_w:
-        cp.start()
-    own_cot.start()
+    own_feat = pltpu.make_async_copy(feat_in, feat, loc_sem.at[3])
+    own_edge = pltpu.make_async_copy(edge_in, edge, loc_sem.at[4])
 
     barrier = pltpu.get_barrier_semaphore()
     greet = [(s, left), (s, right)]
@@ -66,11 +66,14 @@
     greet += [(s, (r + 2 * k) % R) for k in range(1, Z)]
     for dev in greet:
         pl.semaphore_signal(barrier, inc=1, device_id=dev, device_id_type=pl.DeviceIdType.MESH)
+    for cp in [own_feat] + own_w + [own_edge, own_cot]:
+        cp.start()
 
     limit = cnt[0, r]
     rows = lax.broadcasted_iota(jnp.int32, (ROWS, D), 0)
     mask_ref[...] = (rows < limit).astype(F32)
     mask = lambda: mask_ref[...]
+    own_feat.wait()
     h0 = jnp.where(mask() > 0, feat[...], jnp.zeros((ROWS, D), BF))
     hn[0, 0] = h0
     pl.semaphore_wait(barrier, len(greet))
@@ -106,6 +109,7 @@
         for cp in second:
             cp.start()
 
+    own_edge.wait()
     for b in range(2):
         blk = pl.ds(b * BLK, BLK)
         tiles = [edge[b, k] for k in range(3)]
@@ -242,13 +246,13 @@
         sg = jax.nn.sigmoid(p)
         sl = (masked * (sg * (1.0 + p * (1.0 - sg)))).astype(BF)
         slope[l] = sl
-        go(rc(slope.at[l], pslope.at[l], ps_s.at[l], ps_r.at[l], (s, partner)))
         scaled = (mm(sl, w[l, 1], 1, 1) * inv_ref[...]).astype(BF)
         bs[l] = mm(a_halo[...], scaled, 0, 0).astype(BF)
         go(rc(bs.at[l, pl.ds(0, BLK)], bh.at[l, pl.ds(BLK, BLK)],
               bh_s.at[l, 0], bh_r.at[l, 1], (s, left)))
         go(rc(bs.at[l, pl.ds(BLK, BLK)], bh.at[l, pl.ds(0, BLK)],
               bh_s.at[l, 1], bh_r.at[l, 0], (s, right)))
+        go(rc(slope.at[l], pslope.at[l], ps_s.at[l], ps_r.at[l], (s, partner)))
         total = masked + mm(sl, w[l, 0], 1, 1) + mm(a_own[...], scaled, 0, 0)
         stage_b(l)
         stage(stage_c, l + LAG)
@@ -297,6 +301,25 @@
                 to_partner(l, h).wait_send()
 
 
+def emit(scale, final, igrad, gs, gn, final_out, igrad_out, gs_out, gn_out, wide, sem):
+    copies = [
+        pltpu.make_async_copy(final, final_out.at[0], sem.at[0]),
+        pltpu.make_async_copy(igrad, igrad_out.at[0], sem.at[1]),
+    ]
+    for cp in copies:
+        cp.start()
+    step = gs.shape[0] // PARTS
+    for m, (src, dst) in enumerate(((gs, gs_out), (gn, gn_out))):
+        for i in range(PARTS):
+            part = pl.ds(i * step, step)
+            wide[m, part] = src[part].astype(F32) * scale
+            cp = pltpu.make_async_copy(wide.at[m, part], dst.at[0, part], sem.at[2 + m * PARTS + i])
+            cp.start()
+            copies.append(cp)
+    for cp in copies:
+        cp.wait()
+
+
 def body(features, edge_weights, adjacency, counts, weight_self, weight_neighbour, cotangent):
     R, S = lax.axis_size("region"), lax.axis_size("segment")
     rows, D = features.shape[1:]
@@ -312,22 +335,19 @@
     vm = pl.BlockSpec(memory_space=pltpu.VMEM)
     sm = pl.BlockSpec(memory_space=pltpu.SMEM)
     anys = pl.BlockSpec(memory_space=pl.ANY)
-    sems = [DMA((3,))]
+    sems = [DMA((5,))]
     for shape in [((6,), (L, 2)), ((L, 2),) * 2, ((L, 2),) * 2, ((L, 2),) * 2, ((L,),) * 2, ((L,),) * 2,
                   ((L, Q, S - 1),) * 2, ((L, Q, Z - 1),) * 2, ((L, Q, Z - 1),) * 2, ((Q, S),) * 2, ((Q, S),) * 2]:
         sems += [DMA(shape[0]), DMA(shape[1])]
     final, igrad, gs, gn = pl.pallas_call(
         functools.partial(kernel, S, R),
         out_shape=(
-            jax.ShapeDtypeStruct((rows, D), BF),
-            jax.ShapeDtypeStruct((rows, D), BF),
-            jax.ShapeDtypeStruct((D, D), BF),
-            jax.ShapeDtypeStruct((D, D), BF),
+            V((rows, D), BF), V((rows, D), BF), V((D, D), BF), V((D, D), BF),
         ),
-        in_specs=[sm, sm, vm, vm, anys, anys, anys],
+        in_specs=[sm, sm, anys, anys, anys, anys, anys],
         out_specs=(vm, vm, vm, vm),
         scratch_shapes=[
-            V((S, 2, D, D), BF), V((rows, D), BF), V((L, 2, rows, D), BF), V((L, rows, D), F32),
+            V((rows, D), BF), V(edge_weights.shape[1:], BF), V((S, 2, D, D), BF), V((rows, D), BF), V((L, 2, rows, D), BF), V((L, rows, D), F32),
             V((L, 2 * blk, D), BF), V((L, 2 * blk, D), BF), V((L, 2 * blk, D), BF),
             V((L, rows, D), BF), V((L, rows, D), BF), V((L, rows, D), BF),
             V((L, Q, S, CH, D // Q), BF), V((L, Q, S - 1, CH, D // Q), BF),
@@ -340,7 +360,21 @@
         ),
         name="network",
     )(adjacency[0], counts, features[0], edge_weights[0], weight_self[0], weight_neighbour[0], cotangent[0])
-    return (final[None], igrad[None], gs[None].astype(F32) * scale, gn[None].astype(F32) * scale)
+    outs = pl.pallas_call(
+        functools.partial(emit, scale),
+        out_shape=(
+            jax.ShapeDtypeStruct((1, rows, D), BF),
+            jax.ShapeDtypeStruct((1, rows, D), BF),
+            jax.ShapeDtypeStruct((1, D, D), F32),
+            jax.ShapeDtypeStruct((1, D, D), F32),
+        ),
+        in_specs=[vm] * 4,
+        out_specs=(anys,) * 4,
+        scratch_shapes=[V((2, D, D), F32), DMA((2 + 2 * PARTS,))],
+        compiler_params=pltpu.CompilerParams(vmem_limit_bytes=8 * 1024 * 1024),
+        name="emit",
+    )(final, igrad, gs, gn)
+    return tuple(outs)
 
 
 def solution(mesh):

time: 97.1 us -> 92.2 us (0.950)
  other arithmetic: 2.85 us -> 0 us
  local copies, waits for them, and re-layouts: 1.75 us -> 0 us
    mul x1 -> x0, other arithmetic: 2.85 us -> none  [body(): gn[None].astype(F32) * scale]
    unnamed x6 -> x0, local copies, waits for them, and re-layouts: 1.75 us -> none
    pallas_call x1 -> x2, Pallas kernels: 91.7 us -> 91.3 us  [the longest x1 89.8 us: body(): pl.pallas_call(functools.partial(kernel, S, R), out_shape=(V((rows, D), B...]
where the time goes in v1:
time: 92.2 us; the launch traced here: 92 us
  Pallas kernels  91.3 us (99%)
    pallas_call x1, Pallas kernels, body(): pl.pallas_call(functools.partial(kernel, S, R), out_shape=(V((rows, D), B...  89.8 us

profile of v1, /device:TPU:1, one launch (start us, length us, event | category | flops | bytes accessed | tf_op | source)
XLA Modules:
  0.0 92.0 jit_solution(17459549095539397115)
XLA Ops:
  0.6 89.8 %network.1 = (bf16[256,512]{1,0:T(8,128)(2,1)S(1)}, bf16[256,512]{1,0:T(8,128)(2,1)S(1)}, bf16[512,512]{1,0:T(8,128)(2,1)S(1)}, bf16[512,512]{1,0:T(8,128)(2,1)S(1)}) custom-call(s32[2,3]{1,0:T(2,128)} %bitcast.11, s32[1,8]{1,0:T(1,128)} %cnt.1, bf16[256,512]{1,0:T(8,128)(2,1)} %bitcast.8, bf16[2,3,128,128]{3,2,1,0:T(8,128)(2,1)} %bitcast.10, ...), custom_call_target="tpu_custom_call" | custom-call | tf_op jit(solution)/shard_map/network/pallas_call | solution.py:342
  90.4 1.6 %emit.1 = (bf16[1,256,512]{2,1,0:T(8,128)(2,1)}, bf16[1,256,512]{2,1,0:T(8,128)(2,1)}, f32[1,512,512]{2,1,0:T(8,128)}, f32[1,512,512]{2,1,0:T(8,128)}) custom-call(bf16[256,512]{1,0:T(8,128)(2,1)S(1)} %get-tuple-element.8.final, bf16[256,512]{1,0:T(8,128)(2,1)S(1)} %get-tuple-element.9.igrad, bf16[512,512]{1,0:T(8,128)(2,1)S(1)} %get-tuple-element.10.gs, ...), custom_call_target="tpu_custom_call" | custom-call | tf_op jit(solution)/shard_map/emit/pallas_call | solution.py:363

commit v2 on v1

--- a/solution.py
+++ b/solution.py
@@ -9,7 +9,7 @@
 from jax.sharding import PartitionSpec as P
 
 BF = jnp.bfloat16
-LAG = 1
+PLAN = ((0, 1), (1, 2), (2, 3), (3, 4))
 PARTS = 4
 F32 = jnp.float32
 
@@ -30,7 +30,8 @@
     ROWS, D = feat.shape
     CH = D // S
     Q, DQ = zs.shape[1], D // zs.shape[1]
-    pr, pc = zs.shape[3:]
+    tree = Z == 4
+    pr, pc = zs.shape[-2:]
     cols = DQ // pc
     HD = D // 2
     s, r = lax.axis_index("segment"), lax.axis_index("region")
@@ -195,12 +196,33 @@
                 go(rc(gsend.at[l, q, (s + k) % S], srecv.at[l, q, k - 1],
                       sg_s.at[l, q, k - 1], sg_r.at[l, q, k - 1], ((s + k) % S, r)))
 
+    end = (z == 0) | (z == Z - 1)
+    inner = jnp.where(z < 2, 1, 2)
+    outer = jnp.where(z < 2, 0, 3)
+
+    def to_mid(l, q):
+        return rc(zs.at[l, q], zrecv.at[l, q, 0], zr_s.at[l, q, 0], zr_r.at[l, q, 0], (s, 2 * inner + c))
+
+    def across(l, q):
+        return rc(zs.at[l, q], zrecv.at[l, q, 1], zr_s.at[l, q, 1], zr_r.at[l, q, 1], (s, 2 * (3 - inner) + c))
+
+    def to_end(l, q):
+        return rc(zg.at[l, q], zg.at[l, q], zg_s.at[l, q, 0], zg_r.at[l, q, 0], (s, 2 * outer + c))
+
     def stage_c(l, q):
         acc = gsend[l, q, s].astype(F32)
         for k in range(1, S):
             x = srecv.at[l, q, k - 1]
             rc(x, x, sg_s.at[l, q, k - 1], sg_r.at[l, q, k - 1], ((s + k) % S, r)).wait_recv()
             acc = acc + srecv[l, q, k - 1].astype(F32)
+        if tree:
+            zs[l, q] = acc.astype(BF)
+
+            @pl.when(end)
+            def _():
+                to_mid(l, q).start()
+
+            return
         acc = acc.astype(BF)
         for i in range(Z):
             a, b = (i // cols) * pr, (i % cols) * pc
@@ -210,6 +232,14 @@
                   zr_s.at[l, q, k - 1], zr_r.at[l, q, k - 1], (s, (r + 2 * k) % R)))
 
     def stage_d(l, q):
+        if tree:
+            @pl.when(jnp.logical_not(end))
+            def _():
+                to_mid(l, q).wait_recv()
+                zs[l, q] = (zs[l, q].astype(F32) + zrecv[l, q, 0].astype(F32)).astype(BF)
+                across(l, q).start()
+
+            return
         acc = zs[l, q, z].astype(F32)
         for k in range(1, Z):
             x = zrecv.at[l, q, k - 1]
@@ -225,6 +255,18 @@
         return rc(zg.at[l, q], mv.at[s, q], mv_s.at[q, i], mv_r.at[q, i], (l, r))
 
     def stage_e(l, q):
+        if tree:
+            @pl.when(jnp.logical_not(end))
+            def _():
+                across(l, q).wait_recv()
+                zg[l, q] = (zs[l, q].astype(F32) + zrecv[l, q, 1].astype(F32)).astype(BF)
+                to_end(l, q).start()
+
+                @pl.when(s != l)
+                def _():
+                    move(l, q).start()
+
+            return
         for k in range(1, Z):
             x = zg.at[l, q, (z + Z - k) % Z]
             rc(x, x, zg_s.at[l, q, k - 1], zg_r.at[l, q, k - 1], (s, (r + 2 * k) % R)).wait_recv()
@@ -232,6 +274,16 @@
         @pl.when(s != l)
         def _():
             move(l, q).start()
+
+    def stage_f(l, q):
+        if tree:
+            @pl.when(end)
+            def _():
+                to_end(l, q).wait_recv()
+
+                @pl.when(s != l)
+                def _():
+                    move(l, q).start()
 
     def stage(f, l):
         if l < L:
@@ -255,17 +307,17 @@
         go(rc(slope.at[l], pslope.at[l], ps_s.at[l], ps_r.at[l], (s, partner)))
         total = masked + mm(sl, w[l, 0], 1, 1) + mm(a_own[...], scaled, 0, 0)
         stage_b(l)
-        stage(stage_c, l + LAG)
-        stage(stage_d, l + LAG + 1)
-        stage(stage_e, l + LAG + 2)
+        for f, lag in PLAN:
+            stage((stage_c, stage_d, stage_e, stage_f)[f], l + lag)
         halo_wait(l, bh, bh_r)
         grad = (total + bh[l].astype(F32)).astype(BF).astype(F32)
     igrad[...] = (mask() * grad).astype(BF)
 
-    for l in range(-1, -LAG - 3, -1):
-        for f, m in ((stage_e, l + LAG + 2), (stage_d, l + LAG + 1), (stage_c, l + LAG)):
-            if 0 <= m:
-                stage(f, m)
+    lags = dict(PLAN)
+    for l in range(-1, -1 - max(lags.values()), -1):
+        for f, lag in reversed(PLAN):
+            if l + lag >= 0:
+                stage((stage_c, stage_d, stage_e, stage_f)[f], l + lag)
 
     def pair(k, q):
         x = (s + S - k) % S
@@ -283,13 +335,27 @@
             pair(k, q).wait_recv()
     for q in range(Q):
         for k in range(S):
-            for i in range(Z):
+            for i in range(1 if tree else Z):
                 a, b = k * CH + (i // cols) * pr, q * DQ + (i % cols) * pc
-                mine, other = mv[k, q, i], pm[k, q, i]
+                mine, other = (mv[k, q], pm[k, q]) if tree else (mv[k, q, i], pm[k, q, i])
                 gs[pl.ds(a, pr), pl.ds(b, pc)] = jnp.where(c == 0, mine, other)
                 gn[pl.ds(a, pr), pl.ds(b, pc)] = jnp.where(c == 0, other, mine)
     for cp in pending:
         cp.wait_send()
+    if tree:
+        @pl.when(end)
+        def _():
+            for l in range(L):
+                for q in range(Q):
+                    to_mid(l, q).wait_send()
+
+        @pl.when(jnp.logical_not(end))
+        def _():
+            for l in range(L):
+                for q in range(Q):
+                    across(l, q).wait_send()
+                    to_end(l, q).wait_send()
+
     for l in range(L):
         @pl.when(s != l)
         def _():
@@ -329,6 +395,7 @@
     rg = min(Z, CH // 16)
     cg = Z // rg
     pr, pc = CH // rg, D // Q // cg
+    piece, got = ((CH, D // Q), (2, CH, D // Q)) if Z == 4 else ((Z, pr, pc), (Z - 1, pr, pc))
     scale = 1.0 / math.sqrt(S * features.shape[0] * rows * R)
     V = pltpu.VMEM
     DMA = pltpu.SemaphoreType.DMA
@@ -351,8 +418,8 @@
             V((L, 2 * blk, D), BF), V((L, 2 * blk, D), BF), V((L, 2 * blk, D), BF),
             V((L, rows, D), BF), V((L, rows, D), BF), V((L, rows, D), BF),
             V((L, Q, S, CH, D // Q), BF), V((L, Q, S - 1, CH, D // Q), BF),
-            V((L, Q, Z, pr, pc), BF), V((L, Q, Z - 1, pr, pc), BF), V((L, Q, Z, pr, pc), BF),
-            V((S, Q, Z, pr, pc), BF), V((S, Q, Z, pr, pc), BF),
+            V((L, Q, *piece), BF), V((L, Q, *got), BF), V((L, Q, *piece), BF),
+            V((S, Q, *piece), BF), V((S, Q, *piece), BF),
             V((rows, 2 * blk), BF), V((rows, 2 * blk), BF), V((rows, D), F32), V((rows, D), F32),
         ] + sems,
         compiler_params=pltpu.CompilerParams(

time: 92.2 us -> 87.3 us (0.947)
  Pallas kernels: 91.3 us -> 86.5 us
    pallas_call x1, Pallas kernels: 89.8 us -> 84.9 us  [body(): pl.pallas_call(functools.partial(kernel, S, R), out_shape=(V((rows, D), B...]
where the time goes in v2:
time: 87.3 us; the launch traced here: 87.1 us
  Pallas kernels  86.5 us (99%)
    pallas_call x1, Pallas kernels, body(): pl.pallas_call(functools.partial(kernel, S, R), out_shape=(V((rows, D), B...  84.9 us

profile of v2, /device:TPU:1, one launch (start us, length us, event | category | flops | bytes accessed | tf_op | source)
XLA Modules:
  0.0 87.1 jit_solution(14479034777381491750)
XLA Ops:
  0.6 84.9 %network.1 = (bf16[256,512]{1,0:T(8,128)(2,1)S(1)}, bf16[256,512]{1,0:T(8,128)(2,1)S(1)}, bf16[512,512]{1,0:T(8,128)(2,1)S(1)}, bf16[512,512]{1,0:T(8,128)(2,1)S(1)}) custom-call(s32[2,3]{1,0:T(2,128)} %bitcast.11, s32[1,8]{1,0:T(1,128)} %cnt.1, bf16[256,512]{1,0:T(8,128)(2,1)} %bitcast.8, bf16[2,3,128,128]{3,2,1,0:T(8,128)(2,1)} %bitcast.10, ...), custom_call_target="tpu_custom_call" | custom-call | tf_op jit(solution)/shard_map/network/pallas_call | solution.py:409
  85.5 1.6 %emit.1 = (bf16[1,256,512]{2,1,0:T(8,128)(2,1)}, bf16[1,256,512]{2,1,0:T(8,128)(2,1)}, f32[1,512,512]{2,1,0:T(8,128)}, f32[1,512,512]{2,1,0:T(8,128)}) custom-call(bf16[256,512]{1,0:T(8,128)(2,1)S(1)} %get-tuple-element.8.final, bf16[256,512]{1,0:T(8,128)(2,1)S(1)} %get-tuple-element.9.igrad, bf16[512,512]{1,0:T(8,128)(2,1)S(1)} %get-tuple-element.10.gs, ...), custom_call_target="tpu_custom_call" | custom-call | tf_op jit(solution)/shard_map/emit/pallas_call | solution.py:430
